TPU v7x, 32 devices: a whole 2x2x4 slice. The times are simulated.
32 devices in a mesh: gx: 4 (over z), gy: 8 (over y, x, core).
Axes of the slice: x: 2, y: 2, z: 4, core: 2. Of those that a mesh axis runs over, the one named last changes fastest.
Arguments:
- flow: float32 [19, 32, 64, 512], P(None, 'gx', 'gy'), may hold values from 0.0116 to 0.467, as said below
- field: float32 [7, 32, 64, 512], P(None, 'gx', 'gy'), may hold values from -0.45 to 0.45, as said below
- adj_flow_in: float32 [19, 32, 64, 512], P(None, 'gx', 'gy'), may hold values from -6 to 6
- adj_field_in: float32 [7, 32, 64, 512], P(None, 'gx', 'gy'), may hold values from -6 to 6
- profile: float32 [32, 64, 512], P('gx', 'gy'), may hold values from 0.5 to 1.5
- strengths: float32 [32], replicated, may hold values from 0.5 to 2
- wall: int32 [32, 64, 512], P('gx', 'gy'), may hold values 0 or 1
- magnet: int32 [32, 64, 512], P('gx', 'gy'), may hold values from 0 to 31
Outputs:
- new_flow: float32 [19, 32, 64, 512], P(None, 'gx', 'gy')
- new_field: float32 [7, 32, 64, 512], P(None, 'gx', 'gy')
- adj_flow: float32 [19, 32, 64, 512], P(None, 'gx', 'gy')
- adj_field: float32 [7, 32, 64, 512], P(None, 'gx', 'gy')
- magnet_grad: float32 [32], replicated
Inputs may be any that keep to these rules, and one draw needn't show every extreme that they name: flow populations are positive, near w_i times a density of order one. field populations are v_k times a local field value plus noise.
All inputs are finite; a program needn't handle non-finite values. No bound on the sum of `wall` on one device may be relied on, other than what follows from the above.
Results may differ from a plain program's by a relative error of at most 0.00023.
Values sent between devices are 32-bit elements; how exact they have to be, the bound alone decides.
No kernel may reach another device: no remote copies, remote signals or barrier semaphores. Data moves between devices by JAX's collectives and lax.ppermute only.
A program may use at most 64 MiB of HBM per device.

v0:
```python
import math
import jax
import jax.numpy as jnp
import numpy as np
from jax import lax
from jax.sharding import PartitionSpec as P

LATTICE = np.array(
    [
        [0, 0, 0],
        [1, 0, 0],
        [-1, 0, 0],
        [0, 1, 0],
        [0, -1, 0],
        [0, 0, 1],
        [0, 0, -1],
        [1, 1, 0],
        [-1, -1, 0],
        [1, -1, 0],
        [-1, 1, 0],
        [1, 0, 1],
        [-1, 0, -1],
        [1, 0, -1],
        [-1, 0, 1],
        [0, 1, 1],
        [0, -1, -1],
        [0, 1, -1],
        [0, -1, 1],
    ]
)
OPPOSITE = [0, 2, 1, 4, 3, 6, 5, 8, 7, 10, 9, 12, 11, 14, 13, 16, 15, 18, 17]
WEIGHTS_FLOW = [1.0 / 3.0] + [1.0 / 18.0] * 6 + [1.0 / 36.0] * 12
WEIGHTS_FIELD = [0.25] + [0.125] * 6
OMEGA_PLUS = 1.25
OMEGA_MINUS = 1.0 / 1.125
TAU_PLUS = 0.8
COUPLE = 2.0
SOURCE = 2.0


def with_halo(block, sides, width):
    for axis, dim in sides:
        count = lax.axis_size(axis)
        forward = [(i, i + 1) for i in range(count - 1)]
        forward.append((count - 1, 0))
        backward = [(target, source) for source, target in forward]
        low = lax.ppermute(
            lax.slice_in_dim(block, block.shape[dim] - width, None, axis=dim), axis, forward
        )
        high = lax.ppermute(lax.slice_in_dim(block, 0, width, axis=dim), axis, backward)
        block = jnp.concatenate([low, block, high], axis=dim)
    return block


def column(values, ndim):
    return jnp.array([float(v) for v in values], jnp.float32).reshape(
        (len(values),) + (1,) * (ndim - 1)
    )


def collide(flow, field, bfield, fluid):
    ndim = flow.ndim
    velx = column(LATTICE[:, 0], ndim)
    vely = column(LATTICE[:, 1], ndim)
    velz = column(LATTICE[:, 2], ndim)
    weight = column(WEIGHTS_FLOW, ndim)
    weight_b = column(WEIGHTS_FIELD, ndim)
    rho = jnp.sum(flow, 0) + (1.0 - fluid)
    momx = jnp.sum(velx * flow, 0)
    momy = jnp.sum(vely * flow, 0)
    momz = jnp.sum(velz * flow, 0)
    speed_x = momx / rho
    speed_y = momy / rho
    speed_z = momz / rho
    bvalue = jnp.sum(field, 0)
    current = jnp.sum(vely[:7] * field, 0) - bvalue * speed_y
    shear = jnp.sum(velx * vely * flow, 0) - momx * speed_y
    force = COUPLE * bfield * current
    shifted = speed_x + TAU_PLUS * force / rho
    along = velx * shifted + vely * speed_y + velz * speed_z
    square = shifted * shifted + speed_y * speed_y + speed_z * speed_z
    equil = weight * rho * (1.0 + 3.0 * along + 4.5 * along * along - 1.5 * square)
    offset = flow - equil
    flipped = jnp.stack([offset[k] for k in OPPOSITE], 0)
    post_flow = (
        flow - 0.5 * OMEGA_PLUS * (offset + flipped) - 0.5 * OMEGA_MINUS * (offset - flipped)
    )
    along_b = velx[:7] * speed_x + vely[:7] * speed_y + velz[:7] * speed_z
    post_field = weight_b * bvalue * (1.0 + 4.0 * along_b) + weight_b * SOURCE * bfield * shear
    return (post_flow, post_field)


def pull_stream(pad_pops, pad_fluid, post, fluid, count):
    size_x, size_y, size_z = fluid.shape
    parts = []
    for i in range(count):
        cx, cy, cz = (int(v) for v in LATTICE[i])
        near = pad_fluid[
            1 - cx : 1 - cx + size_x, 1 - cy : 1 - cy + size_y, 1 - cz : 1 - cz + size_z
        ]
        moved = pad_pops[
            i, 1 - cx : 1 - cx + size_x, 1 - cy : 1 - cy + size_y, 1 - cz : 1 - cz + size_z
        ]
        parts.append(fluid * (near * moved + (1.0 - near) * post[OPPOSITE[i]]))
    return jnp.stack(parts, 0)


def push_adjoint(pad_pops, pad_fluid, local, fluid, count):
    size_x, size_y, size_z = fluid.shape
    parts = []
    for i in range(count):
        cx, cy, cz = (int(v) for v in LATTICE[i])
        near = pad_fluid[
            1 + cx : 1 + cx + size_x, 1 + cy : 1 + cy + size_y, 1 + cz : 1 + cz + size_z
        ]
        moved = pad_pops[
            i, 1 + cx : 1 + cx + size_x, 1 + cy : 1 + cy + size_y, 1 + cz : 1 + cz + size_z
        ]
        parts.append(fluid * (near * moved + (1.0 - near) * local[OPPOSITE[i]]))
    return jnp.stack(parts, 0)


def close_ends(padded):
    return jnp.pad(padded, ((0, 0), (0, 0), (0, 0), (1, 1)))


def wall_rims(pad_fluid):
    rows = lax.broadcasted_iota(jnp.int32, pad_fluid.shape, 1)
    here = lax.axis_index("gy")
    last = lax.axis_size("gy") - 1
    outside = (rows == 0) & (here == 0) | (rows == pad_fluid.shape[1] - 1) & (here == last)
    return jnp.where(outside, 0.0, pad_fluid)


def on_device(flow, field, adj_flow_in, adj_field_in, profile, strengths, wall, magnet):
    count_mag = strengths.shape[0]
    fluid = (1 - wall).astype(jnp.float32)
    table = (
        magnet[None] == lax.broadcasted_iota(jnp.int32, (count_mag,) + magnet.shape, 0)
    ).astype(jnp.float32)
    bcell = jnp.tensordot(strengths, table, axes=1, precision=lax.Precision.HIGHEST) * profile
    post_flow, post_field = collide(flow, field, bcell, fluid)
    joined = jnp.concatenate([post_flow, post_field, fluid[None]], 0)
    padded = close_ends(with_halo(joined, (("gx", 1), ("gy", 2)), 1))
    pad_fluid = wall_rims(padded[26])
    pad_state = padded[:26]
    incoming = jnp.concatenate([adj_flow_in, adj_field_in], 0)
    pad_adj = close_ends(with_halo(incoming, (("gx", 1), ("gy", 2)), 1))
    new_flow = pull_stream(pad_state[:19], pad_fluid, post_flow, fluid, 19)
    new_field = pull_stream(pad_state[19:], pad_fluid, post_field, fluid, 7)
    ast_flow = push_adjoint(pad_adj[:19], pad_fluid, adj_flow_in, fluid, 19)
    ast_field = push_adjoint(pad_adj[19:], pad_fluid, adj_field_in, fluid, 7)

    def local_collide(first, second, third):
        return collide(first, second, third, fluid)

    _, pullback = jax.vjp(local_collide, new_flow, new_field, bcell)
    adj_flow, adj_field, dcell = pullback((ast_flow, ast_field))
    shares = jnp.tensordot(table, dcell * profile, axes=3, precision=lax.Precision.HIGHEST)
    totals = lax.psum(shares, ("gx", "gy"))
    cells = (
        flow.shape[1] * lax.axis_size("gx") * flow.shape[2] * lax.axis_size("gy") * flow.shape[3]
    )
    magnet_grad = totals / math.sqrt(cells / count_mag)
    return (new_flow, new_field, adj_flow, adj_field, magnet_grad)


def solution(mesh):
    return jax.shard_map(
        on_device,
        mesh=mesh,
        in_specs=(
            P(None, "gx", "gy", None),
            P(None, "gx", "gy", None),
            P(None, "gx", "gy", None),
            P(None, "gx", "gy", None),
            P("gx", "gy", None),
            P(),
            P("gx", "gy", None),
            P("gx", "gy", None),
        ),
        out_specs=(
            P(None, "gx", "gy", None),
            P(None, "gx", "gy", None),
            P(None, "gx", "gy", None),
            P(None, "gx", "gy", None),
            P(),
        ),
        check_vma=False,
    )
```

profile of v0, /device:TPU:0, one launch (start us, length us, event | category | flops | bytes accessed | tf_op | source)
XLA Modules:
  0.0 164.3 jit_solution(2467456283072510997)
XLA Ops:
  0.7 2.0 %constant_dynamic-update-slice_fusion.46 = f32[26,8,8,512]{3,2,1,0:T(8,128)S(1)} fusion(f32[19,8,8,512]{3,2,1,0:T(8,128)} %param.20), kind=kLoop, calls=%fused_computation.129 | loop fusion | bytes 4980736
  2.8 1.0 fusion.254
  3.8 3.0 %collective-permute-start.5 = (f32[26,1,8,512]{3,2,1,0:T(8,128)}, f32[26,1,8,512]{3,2,1,0:T(8,128)}, u32[]{:S(2)}, u32[]{:S(2)}) collective-permute-start(f32[26,1,8,512]{3,2,1,0:T(8,128)} %get-tuple-element.112), channel_id=1, source_target_pairs={{0,8},{8,16},{16,24},{24,0},{1,9},{9,17},{17,25},{25,1},{2,10},{10... | collective-permute-start | bytes 1277960 | tf_op jit(solution)/shard_map/ppermute | solution.py:47
  6.8 2.1 %collective-permute-start.4 = (f32[26,1,8,512]{3,2,1,0:T(8,128)}, f32[26,1,8,512]{3,2,1,0:T(8,128)}, u32[]{:S(2)}, u32[]{:S(2)}) collective-permute-start(f32[26,1,8,512]{3,2,1,0:T(8,128)} %get-tuple-element.113), channel_id=1, source_target_pairs={{8,0},{16,8},{24,16},{0,24},{9,1},{17,9},{25,17},{1,25},{10,2},{18... | collective-permute-start | bytes 1277960 | tf_op jit(solution)/shard_map/ppermute | solution.py:50
  9.7 1.6 fusion.4
  11.4 1.0 multiply_reduce_fusion.7
  12.6 1.3 fusion.16
  14.3 1.8 %multiply_subtract_fusion = f32[19,8,8,512]{3,2,1,0:T(8,128)S(1)} fusion(f32[19,8,8,512]{3,2,1,0:T(8,128)S(1)} %constant_dynamic-update-slice_fusion, f32[19,8,8,512]{3,2,1,0:T(8,128)S(1)} %copy-done.7, f32[8,8,512]{2,1,0:T(8,128)S(1)} %get-tuple-element.77, f32[8,8,512]{2,1,0:T(8,128)S(1)} %get-tuple-element.81, f32[19]{0:T(128)S(1)} %copy-done.44, ...), kind=kLoop, calls=%fused_computation.48 | loop fusion | flops 12451840 | bytes 8126768 | tf_op jit(solution)/shard_map/sub | solution.py:86
  17.3 1.0 pad_maximum_fusion.10
  18.3 3.8 %collective-permute-start.1 = (f32[27,1,8,512]{3,2,1,0:T(8,128)}, f32[27,1,8,512]{3,2,1,0:T(8,128)}, u32[]{:S(2)}, u32[]{:S(2)}) collective-permute-start(f32[27,1,8,512]{3,2,1,0:T(8,128)} %get-tuple-element.111), channel_id=1, source_target_pairs={{8,0},{16,8},{24,16},{0,24},{9,1},{17,9},{25,17},{1,25},{10,2},{18... | collective-permute-start | bytes 1327112 | tf_op jit(solution)/shard_map/ppermute | solution.py:50
  22.1 7.0 %collective-permute-done.4 = f32[26,1,8,512]{3,2,1,0:T(8,128)} collective-permute-done((f32[26,1,8,512]{3,2,1,0:T(8,128)}, f32[26,1,8,512]{3,2,1,0:T(8,128)}, u32[]{:S(2)}, u32[]{:S(2)}) %collective-permute-start.4) | collective-permute-done | bytes 426016 | tf_op jit(solution)/shard_map/ppermute | solution.py:50
  29.1 4.5 %pad_maximum_fusion.5 = (f32[26,10,1,512]{3,2,1,0:T(1,128)S(1)}, f32[26,10,1,512]{3,2,1,0:T(1,128)S(1)}) fusion(f32[26,1,8,512]{3,2,1,0:T(8,128)} %collective-permute-done.4, f32[26,8,8,512]{3,2,1,0:T(8,128)} %copy-done.2, f32[26,1,8,512]{3,2,1,0:T(8,128)} %collective-permute-done.5), kind=kLoop, calls=%fused_computation.72 | loop fusion | flops 532480 | bytes 5324800 | tf_op jit(solution)/shard_map/concatenate | solution.py:51
  33.7 2.6 %collective-permute-start.6 = (f32[26,10,1,512]{3,2,1,0:T(1,128)S(1)}, f32[26,10,1,512]{3,2,1,0:T(1,128)S(1)}, u32[]{:S(2)}, u32[]{:S(2)}) collective-permute-start(f32[26,10,1,512]{3,2,1,0:T(1,128)S(1)} %get-tuple-element.109), channel_id=1, source_target_pairs={{1,0},{2,1},{3,2},{4,3},{5,4},{6,5},{7,6},{0,7},{9,8},{10,9},{11,1... | collective-permute-start | bytes 1597448 | tf_op jit(solution)/shard_map/ppermute | solution.py:50
  36.3 2.2 %collective-permute-done = f32[27,1,8,512]{3,2,1,0:T(8,128)} collective-permute-done((f32[27,1,8,512]{3,2,1,0:T(8,128)}, f32[27,1,8,512]{3,2,1,0:T(8,128)}, u32[]{:S(2)}, u32[]{:S(2)}) %collective-permute-start) | collective-permute-done | bytes 442400 | tf_op jit(solution)/shard_map/ppermute | solution.py:47
  38.5 8.1 %collective-permute-done.1 = f32[27,1,8,512]{3,2,1,0:T(8,128)} collective-permute-done((f32[27,1,8,512]{3,2,1,0:T(8,128)}, f32[27,1,8,512]{3,2,1,0:T(8,128)}, u32[]{:S(2)}, u32[]{:S(2)}) %collective-permute-start.1) | collective-permute-done | bytes 442400 | tf_op jit(solution)/shard_map/ppermute | solution.py:50
  46.6 2.2 %pad_maximum_fusion.4 = (f32[27,10,1,512]{3,2,1,0:T(1,128)S(1)}, f32[27,10,1,512]{3,2,1,0:T(1,128)S(1)}) fusion(f32[27,1,8,512]{3,2,1,0:T(8,128)} %collective-permute-done.1, f32[27,1,8,512]{3,2,1,0:T(8,128)} %collective-permute-done, f32[1,8,8,512]{3,2,1,0:T(8,128)S(1)} %copy-done.9, f32[7,8,8,512]{3,2,1,0:T(8,128)S(1)} %fusion.21, ...), kind=kLoop, calls=%fused_computation.71 | loop fusion | flops 1105920 | bytes 5529600 | tf_op jit(solution)/shard_map/slice | solution.py:48
  48.8 2.6 %collective-permute-start.3 = (f32[27,10,1,512]{3,2,1,0:T(1,128)S(1)}, f32[27,10,1,512]{3,2,1,0:T(1,128)S(1)}, u32[]{:S(2)}, u32[]{:S(2)}) collective-permute-start(f32[27,10,1,512]{3,2,1,0:T(1,128)S(1)} %get-tuple-element.103), channel_id=1, source_target_pairs={{1,0},{2,1},{3,2},{4,3},{5,4},{6,5},{7,6},{0,7},{9,8},{10,9},{11,1... | collective-permute-start | bytes 1658888 | tf_op jit(solution)/shard_map/ppermute | solution.py:50
  51.5 13.1 %select_maximum_fusion.6 = f32[26,10,10,514]{3,2,1,0:T(8,128)S(1)} fusion(f32[26,10,1,512]{3,2,1,0:T(1,128)S(1)} %collective-permute-done.6, f32[26,10,1,512]{3,2,1,0:T(1,128)S(1)} %collective-permute-done.7, f32[26,1,8,512]{3,2,1,0:T(8,128)} %collective-permute-done.4, f32[26,8,8,512]{3,2,1,0:T(8,128)S(1)} %copy-done.3, ...), kind=kLoop, calls=%fused_computation.11 | loop fusion | flops 16036800 | bytes 10670400 | tf_op jit(solution)/shard_map/concatenate | solution.py:51
  64.6 21.7 %select_maximum_fusion = f32[27,10,10,514]{3,2,1,0:T(8,128)S(1)} fusion(f32[27,10,1,512]{3,2,1,0:T(1,128)S(1)} %collective-permute-done.3, f32[27,10,1,512]{3,2,1,0:T(1,128)S(1)} %collective-permute-done.2, f32[27,1,8,512]{3,2,1,0:T(8,128)} %collective-permute-done.1, f32[27,1,8,512]{3,2,1,0:T(8,128)} %collective-permute-done, ...), kind=kLoop, calls=%fused_computation.4 | loop fusion | flops 22204800 | bytes 11080800 | tf_op jit(solution)/shard_map/concatenate | solution.py:51
  91.0 0.9 constant_dynamic-update-slice_fusion.68
  95.2 1.0 constant_dynamic-update-slice_fusion.43
  96.1 0.9 constant_dynamic-update-slice_fusion.42
  104.4 2.6 %fusion.7 = (f32[19,8,8,512]{3,2,1,0:T(8,128)S(1)}, f32[19,8,8,512]{3,2,1,0:T(8,128)S(1)}) fusion(f32[8,8,512]{2,1,0:T(8,128)S(1)} %get-tuple-element.47, f32[8,8,512]{2,1,0:T(8,128)S(1)} %get-tuple-element.40, f32[8,8,512]{2,1,0:T(8,128)S(1)} %get-tuple-element.43, f32[8,8,512]{2,1,0:T(8,128)S(1)} %get-tuple-element.41, f32[19]{0:T(128)S(1)} %copy-done.44, ...), kind=kLoop, calls=%fused_computation.25 | loop fusion | flops 25526272 | bytes 10355011 | tf_op jit(solution)/shard_map/transpose(jvp())/add_any | solution.py:82
  107.1 3.1 %multiply_reduce_fusion.3 = (f32[8,8,512]{2,1,0:T(8,128)}, f32[8,8,512]{2,1,0:T(8,128)S(1)}, f32[8,8,512]{2,1,0:T(8,128)}, f32[8,8,512]{2,1,0:T(8,128)S(1)}, f32[8,8,512]{2,1,0:T(8,128)}) fusion(f32[19,8,8,512]{3,2,1,0:T(8,128)S(1)} %get-tuple-element.48, f32[19]{0:T(128)S(1)} %copy-done.44, f32[19]{0:T(128)S(1)} %copy-done.46, f32[19]{0:T(128)S(1)} %copy-done.45, ...), kind=kLoop, calls=%fused_computation.39 | loop fusion | flops 14778368 | bytes 6291760 | tf_op jit(solution)/shard_map/transpose(jvp())/reduce_sum | solution.py:80
  110.3 1.6 multiply_reduce_fusion.11
  112.6 5.1 %fusion.18 = f32[32]{0:T(128)} fusion(pred[32,8,8,512]{3,2,1,0:T(8,128)(4,1)S(1)} %copy-done.35, f32[8,8,512,1]{2,1,0,3:T(8,128)S(1)} %get-tuple-element.33), kind=kOutput, calls=%fused_computation.55 | convolution fusion | flops 12582912 | bytes 1179776 | tf_op jit(solution)/shard_map/dot_general | solution.py:159
  117.7 39.0 %psum.7 = f32[32]{0:T(128)} all-reduce(f32[32]{0:T(128)} %fusion.18), channel_id=1, replica_groups=mesh['gx'=4,'gy'=8] {'gx','gy'}, use_global_device_ids=true, to_apply=%region_23.24 | all-reduce | flops 32 | bytes 256 | tf_op jit(solution)/shard_map/psum | solution.py:160
  156.8 1.2 broadcast_multiply_fusion
  158.0 1.0 multiply_add_fusion.3
  159.1 1.1 multiply_add_fusion.1
  160.2 1.2 fusion.239
  161.8 2.5 %add_add_fusion = f32[19,8,8,512]{3,2,1,0:T(8,128)} fusion(f32[19,8,8,512]{3,2,1,0:T(8,128)S(1)} %copy-done.6, f32[19,8,8,512]{3,2,1,0:T(8,128)S(1)} %get-tuple-element.49, f32[8,8,512]{2,1,0:T(8,128)S(1)} %get-tuple-element.133, f32[8,8,512]{2,1,0:T(8,128)S(1)} %get-tuple-element.138, f32[8,8,512]{2,1,0:T(8,128)S(1)} %get-tuple-element.37, ...), kind=kLoop, calls=%fused_computation.36 | loop fusion | flops 6225920 | bytes 8126768 | tf_op jit(solution)/shard_map/transpose(jvp())/add_any | solution.py:68
  (210 shorter events, 18.6 us)
Async XLA Ops:
  0.6 9.1 %copy-start = (f32[32]{0:T(128)S(1)}, f32[32]{0:T(128)}, u32[]{:S(2)}) copy-start(f32[32]{0:T(128)} %param.23) | copy-start | bytes 388
  2.7 6.2 %copy-start.43 = (s32[8,8,512]{2,1,0:T(8,128)S(1)}, s32[8,8,512]{2,1,0:T(8,128)}, u32[]{:S(2)}) copy-start(s32[8,8,512]{2,1,0:T(8,128)} %param.25) | copy-start | bytes 393220
  2.7 6.8 %copy-start.36 = (f32[7,8,8,512]{3,2,1,0:T(8,128)S(1)}, f32[7,8,8,512]{3,2,1,0:T(8,128)}, u32[]{:S(2)}) copy-start(f32[7,8,8,512]{3,2,1,0:T(8,128)} %param.19) | copy-start | bytes 2752516
  2.7 6.8 %copy-start.47 = (f32[7]{0:T(128)S(1)}, f32[7]{0:T(128)}, u32[]{:S(2)}) copy-start(f32[7]{0:T(128)} %constant.97) | copy-start | bytes 88
  2.8 8.5 %copy-start.2 = (f32[26,8,8,512]{3,2,1,0:T(8,128)}, f32[26,8,8,512]{3,2,1,0:T(8,128)S(1)}, u32[]{:S(2)}) copy-start(f32[26,8,8,512]{3,2,1,0:T(8,128)S(1)} %constant_dynamic-update-slice_fusion.45) | copy-start | bytes 10223620
  3.8 18.4 %collective-permute-start.5 = (f32[26,1,8,512]{3,2,1,0:T(8,128)}, f32[26,1,8,512]{3,2,1,0:T(8,128)}, u32[]{:S(2)}, u32[]{:S(2)}) collective-permute-start(f32[26,1,8,512]{3,2,1,0:T(8,128)} %get-tuple-element.112), channel_id=1, source_target_pairs={{0,8},{8,16},{16,24},{24,0},{1,9},{9,17},{17,25},{25,1},{2,10},{10... | collective-permute-start | bytes 1277960 | tf_op jit(solution)/shard_map/ppermute | solution.py:47
  6.8 22.3 %collective-permute-start.4 = (f32[26,1,8,512]{3,2,1,0:T(8,128)}, f32[26,1,8,512]{3,2,1,0:T(8,128)}, u32[]{:S(2)}, u32[]{:S(2)}) collective-permute-start(f32[26,1,8,512]{3,2,1,0:T(8,128)} %get-tuple-element.113), channel_id=1, source_target_pairs={{8,0},{16,8},{24,16},{0,24},{9,1},{17,9},{25,17},{1,25},{10,2},{18... | collective-permute-start | bytes 1277960 | tf_op jit(solution)/shard_map/ppermute | solution.py:50
  18.3 20.2 %collective-permute-start = (f32[27,1,8,512]{3,2,1,0:T(8,128)}, f32[27,1,8,512]{3,2,1,0:T(8,128)}, u32[]{:S(2)}, u32[]{:S(2)}) collective-permute-start(f32[27,1,8,512]{3,2,1,0:T(8,128)} %get-tuple-element.110), channel_id=1, source_target_pairs={{0,8},{8,16},{16,24},{24,0},{1,9},{9,17},{17,25},{25,1},{2,10},{10... | collective-permute-start | bytes 1327112 | tf_op jit(solution)/shard_map/ppermute | solution.py:47
  18.3 28.2 %collective-permute-start.1 = (f32[27,1,8,512]{3,2,1,0:T(8,128)}, f32[27,1,8,512]{3,2,1,0:T(8,128)}, u32[]{:S(2)}, u32[]{:S(2)}) collective-permute-start(f32[27,1,8,512]{3,2,1,0:T(8,128)} %get-tuple-element.111), channel_id=1, source_target_pairs={{8,0},{16,8},{24,16},{0,24},{9,1},{17,9},{25,17},{1,25},{10,2},{18... | collective-permute-start | bytes 1327112 | tf_op jit(solution)/shard_map/ppermute | solution.py:50
  22.1 24.4 %copy-start.9 = (f32[1,8,8,512]{3,2,1,0:T(8,128)S(1)}, f32[1,8,8,512]{3,2,1,0:T(8,128)}, u32[]{:S(2)}) copy-start(f32[1,8,8,512]{3,2,1,0:T(8,128)} %copy-done.8) | copy-start | bytes 393220
  33.6 17.9 %collective-permute-start.7 = (f32[26,10,1,512]{3,2,1,0:T(1,128)S(1)}, f32[26,10,1,512]{3,2,1,0:T(1,128)S(1)}, u32[]{:S(2)}, u32[]{:S(2)}) collective-permute-start(f32[26,10,1,512]{3,2,1,0:T(1,128)S(1)} %get-tuple-element.108), channel_id=1, source_target_pairs={{0,1},{1,2},{2,3},{3,4},{4,5},{5,6},{6,7},{7,0},{8,9},{9,10},{10,1... | collective-permute-start | bytes 1597448 | tf_op jit(solution)/shard_map/ppermute | solution.py:47
  33.7 17.8 %collective-permute-start.6 = (f32[26,10,1,512]{3,2,1,0:T(1,128)S(1)}, f32[26,10,1,512]{3,2,1,0:T(1,128)S(1)}, u32[]{:S(2)}, u32[]{:S(2)}) collective-permute-start(f32[26,10,1,512]{3,2,1,0:T(1,128)S(1)} %get-tuple-element.109), channel_id=1, source_target_pairs={{1,0},{2,1},{3,2},{4,3},{5,4},{6,5},{7,6},{0,7},{9,8},{10,9},{11,1... | collective-permute-start | bytes 1597448 | tf_op jit(solution)/shard_map/ppermute | solution.py:50
  36.3 15.2 %copy-start.3 = (f32[26,8,8,512]{3,2,1,0:T(8,128)S(1)}, f32[26,8,8,512]{3,2,1,0:T(8,128)}, u32[]{:S(2)}) copy-start(f32[26,8,8,512]{3,2,1,0:T(8,128)} %copy-done.2) | copy-start | bytes 10223620
  48.8 15.8 %collective-permute-start.2 = (f32[27,10,1,512]{3,2,1,0:T(1,128)S(1)}, f32[27,10,1,512]{3,2,1,0:T(1,128)S(1)}, u32[]{:S(2)}, u32[]{:S(2)}) collective-permute-start(f32[27,10,1,512]{3,2,1,0:T(1,128)S(1)} %get-tuple-element.102), channel_id=1, source_target_pairs={{0,1},{1,2},{2,3},{3,4},{4,5},{5,6},{6,7},{7,0},{8,9},{9,10},{10,1... | collective-permute-start | bytes 1658888 | tf_op jit(solution)/shard_map/ppermute | solution.py:47
  48.8 15.7 %collective-permute-start.3 = (f32[27,10,1,512]{3,2,1,0:T(1,128)S(1)}, f32[27,10,1,512]{3,2,1,0:T(1,128)S(1)}, u32[]{:S(2)}, u32[]{:S(2)}) collective-permute-start(f32[27,10,1,512]{3,2,1,0:T(1,128)S(1)} %get-tuple-element.103), channel_id=1, source_target_pairs={{1,0},{2,1},{3,2},{4,3},{5,4},{6,5},{7,6},{0,7},{9,8},{10,9},{11,1... | collective-permute-start | bytes 1658888 | tf_op jit(solution)/shard_map/ppermute | solution.py:50
  64.5 21.9 %copy-start.10 = (f32[19,8,8,512]{3,2,1,0:T(8,128)S(1)}, f32[19,8,8,512]{3,2,1,0:T(8,128)}, u32[]{:S(2)}) copy-start(f32[19,8,8,512]{3,2,1,0:T(8,128)} %param.20) | copy-start | bytes 7471108
  64.5 21.9 %copy-start.19 = (f32[7,8,8,512]{3,2,1,0:T(8,128)S(1)}, f32[7,8,8,512]{3,2,1,0:T(8,128)}, u32[]{:S(2)}) copy-start(f32[7,8,8,512]{3,2,1,0:T(8,128)} %param.21) | copy-start | bytes 2752516
  94.5 9.7 %copy-start.5 = (f32[19,8,8,512]{3,2,1,0:T(8,128)}, f32[19,8,8,512]{3,2,1,0:T(8,128)S(1)}, u32[]{:S(2)}) copy-start(f32[19,8,8,512]{3,2,1,0:T(8,128)S(1)} %get-tuple-element.87) | copy-start | bytes 7471108
  103.6 6.6 %copy-start.11 = (f32[8,8,512]{2,1,0:T(8,128)}, f32[8,8,512]{2,1,0:T(8,128)S(1)}, u32[]{:S(2)}) copy-start(f32[8,8,512]{2,1,0:T(8,128)S(1)} %get-tuple-element.40) | copy-start | bytes 393220
  103.6 8.3 %copy-start.13 = (f32[8,8,512]{2,1,0:T(8,128)}, f32[8,8,512]{2,1,0:T(8,128)S(1)}, u32[]{:S(2)}) copy-start(f32[8,8,512]{2,1,0:T(8,128)S(1)} %get-tuple-element.41) | copy-start | bytes 393220
  104.2 5.9 %copy-start.20 = (f32[8,8,512]{2,1,0:T(8,128)}, f32[8,8,512]{2,1,0:T(8,128)S(1)}, u32[]{:S(2)}) copy-start(f32[8,8,512]{2,1,0:T(8,128)S(1)} %get-tuple-element.47) | copy-start | bytes 393220
  104.2 5.9 %copy-start.33 = (f32[8,8,512]{2,1,0:T(8,128)}, f32[8,8,512]{2,1,0:T(8,128)S(1)}, u32[]{:S(2)}) copy-start(f32[8,8,512]{2,1,0:T(8,128)S(1)} %get-tuple-element.45) | copy-start | bytes 393220
  104.3 7.6 %copy-start.30 = (f32[8,8,512]{2,1,0:T(8,128)}, f32[8,8,512]{2,1,0:T(8,128)S(1)}, u32[]{:S(2)}) copy-start(f32[8,8,512]{2,1,0:T(8,128)S(1)} %get-tuple-element.44) | copy-start | bytes 393220
  111.9 46.2 %copy-start.12 = (f32[8,8,512]{2,1,0:T(8,128)S(1)}, f32[8,8,512]{2,1,0:T(8,128)}, u32[]{:S(2)}) copy-start(f32[8,8,512]{2,1,0:T(8,128)} %copy-done.11) | copy-start | bytes 393220
  111.9 46.2 %copy-start.17 = (f32[8,8,512]{2,1,0:T(8,128)S(1)}, f32[8,8,512]{2,1,0:T(8,128)}, u32[]{:S(2)}) copy-start(f32[8,8,512]{2,1,0:T(8,128)} %copy-done.15) | copy-start | bytes 393220
  112.6 45.4 %copy-start.14 = (f32[8,8,512]{2,1,0:T(8,128)S(1)}, f32[8,8,512]{2,1,0:T(8,128)}, u32[]{:S(2)}) copy-start(f32[8,8,512]{2,1,0:T(8,128)} %copy-done.13) | copy-start | bytes 393220
  112.6 47.6 %copy-start.23 = (f32[8,8,512]{2,1,0:T(8,128)S(1)}, f32[8,8,512]{2,1,0:T(8,128)}, u32[]{:S(2)}) copy-start(f32[8,8,512]{2,1,0:T(8,128)} %copy-done.22) | copy-start | bytes 393220
  117.7 43.7 %copy-start.21 = (f32[8,8,512]{2,1,0:T(8,128)S(1)}, f32[8,8,512]{2,1,0:T(8,128)}, u32[]{:S(2)}) copy-start(f32[8,8,512]{2,1,0:T(8,128)} %copy-done.20) | copy-start | bytes 393220
  117.7 43.7 %copy-start.27 = (f32[8,8,512]{2,1,0:T(8,128)S(1)}, f32[8,8,512]{2,1,0:T(8,128)}, u32[]{:S(2)}) copy-start(f32[8,8,512]{2,1,0:T(8,128)} %copy-done.26) | copy-start | bytes 393220
  156.8 4.7 %copy-start.38 = (f32[8,8,512]{2,1,0:T(8,128)S(1)}, f32[8,8,512]{2,1,0:T(8,128)}, u32[]{:S(2)}) copy-start(f32[8,8,512]{2,1,0:T(8,128)} %get-tuple-element.32) | copy-start | bytes 393220
  156.8 4.7 %copy-start.39 = (f32[8,8,512]{2,1,0:T(8,128)S(1)}, f32[8,8,512]{2,1,0:T(8,128)}, u32[]{:S(2)}) copy-start(f32[8,8,512]{2,1,0:T(8,128)} %get-tuple-element.26) | copy-start | bytes 393220
  156.8 4.7 %copy-start.40 = (f32[8,8,512]{2,1,0:T(8,128)S(1)}, f32[8,8,512]{2,1,0:T(8,128)}, u32[]{:S(2)}) copy-start(f32[8,8,512]{2,1,0:T(8,128)} %get-tuple-element.28) | copy-start | bytes 393220
  (42 other events, 107.0 us)
where the time goes:
time: 167 us; the launch traced here: 164 us
  other arithmetic  80.1 us (48%)
  blocking collectives  39 us (23%)
  waiting for transfers between devices  17.2 us (10%)
  starting transfers between devices  14.3 us (9%)
  matrix products  6.66 us (4%)
  local copies, waits for them, and re-layouts  4.91 us (3%)
  between operations  1.99 us (1%)
    concatenate x3, other arithmetic, with_halo(): block = jnp.concatenate([low, block, high], axis=dim)  39.2 us
    psum x1, blocking collectives, on_device(): totals = lax.psum(shares, ('gx', 'gy'))  39 us
    ppermute x4, waiting for transfers between devices, with_halo(): lax.ppermute(lax.slice_in_dim(block, 0, width, axis=dim), axis, backward)  15.1 us
    unnamed x35, other arithmetic  14.2 us
    ppermute x4, starting transfers between devices, with_halo(): lax.ppermute(lax.slice_in_dim(block, 0, width, axis=dim), axis, backward)  11.2 us
    dot_general x1, matrix products, on_device(): jnp.tensordot(table, dcell * profile, axes=3, precision=lax.Precision.HIG...  5.09 us
    unnamed x151, local copies, waits for them, and re-layouts  3.65 us
  transfers between devices with their start and end apart: 8, of which 3 were waited for; matrix products, arithmetic and copies ran while one was open for 17% of the time, Pallas kernels for 0%

commit v1 on v0

--- a/solution.py
+++ b/solution.py
@@ -157,7 +157,7 @@
     _, pullback = jax.vjp(local_collide, new_flow, new_field, bcell)
     adj_flow, adj_field, dcell = pullback((ast_flow, ast_field))
     shares = jnp.tensordot(table, dcell * profile, axes=3, precision=lax.Precision.HIGHEST)
-    totals = lax.psum(shares, ("gx", "gy"))
+    totals = lax.psum(lax.psum(shares, "gy"), "gx")
     cells = (
         flow.shape[1] * lax.axis_size("gx") * flow.shape[2] * lax.axis_size("gy") * flow.shape[3]
     )

time: 167 us -> 152 us (0.910)
  blocking collectives: 39 us -> 24.6 us
    psum x1 -> x2, blocking collectives: 39 us -> 24.6 us  [on_device(): totals = lax.psum(lax.psum(shares, 'gy'), 'gx')]
  transfers between devices with their start and end apart: 8 -> 8, of which waited for: 3 -> 3; matrix products, arithmetic and copies ran while one was open for 17% -> 19% of each run, Pallas kernels for 0% -> 0%
where the time goes in v1:
time: 152 us; the launch traced here: 150 us
  other arithmetic  80.2 us (53%)
  blocking collectives  24.6 us (16%)
  waiting for transfers between devices  17.2 us (11%)
  starting transfers between devices  14.3 us (9%)
  matrix products  6.66 us (4%)
  local copies, waits for them, and re-layouts  4.92 us (3%)
  between operations  1.98 us (1%)
    concatenate x3, other arithmetic, with_halo(): block = jnp.concatenate([low, block, high], axis=dim)  39.3 us
    psum x2, blocking collectives, on_device(): totals = lax.psum(lax.psum(shares, 'gy'), 'gx')  24.6 us
    ppermute x4, waiting for transfers between devices, with_halo(): lax.ppermute(lax.slice_in_dim(block, 0, width, axis=dim), axis, backward)  15 us
    unnamed x35, other arithmetic  14.2 us
    ppermute x4, starting transfers between devices, with_halo(): lax.ppermute(lax.slice_in_dim(block, 0, width, axis=dim), axis, backward)  11.2 us
    dot_general x1, matrix products, on_device(): jnp.tensordot(table, dcell * profile, axes=3, precision=lax.Precision.HIG...  5.09 us
    unnamed x151, local copies, waits for them, and re-layouts  3.66 us
    slice x2, other arithmetic, with_halo(): lax.slice_in_dim(block, block.shape[dim] - width, None, axis=dim)  3.17 us
  transfers between devices with their start and end apart: 8, of which 3 were waited for; matrix products, arithmetic and copies ran while one was open for 19% of the time, Pallas kernels for 0%

profile of v1, /device:TPU:0, one launch (start us, length us, event | category | flops | bytes accessed | tf_op | source)
XLA Modules:
  0.0 149.9 jit_solution(9207649444324201465)
XLA Ops:
  0.7 2.0 %constant_dynamic-update-slice_fusion.46 = f32[26,8,8,512]{3,2,1,0:T(8,128)S(1)} fusion(f32[19,8,8,512]{3,2,1,0:T(8,128)} %param.20), kind=kLoop, calls=%fused_computation.129 | loop fusion | bytes 4980736
  2.8 1.0 fusion.254
  3.8 3.0 %collective-permute-start.5 = (f32[26,1,8,512]{3,2,1,0:T(8,128)}, f32[26,1,8,512]{3,2,1,0:T(8,128)}, u32[]{:S(2)}, u32[]{:S(2)}) collective-permute-start(f32[26,1,8,512]{3,2,1,0:T(8,128)} %get-tuple-element.112), channel_id=1, source_target_pairs={{0,8},{8,16},{16,24},{24,0},{1,9},{9,17},{17,25},{25,1},{2,10},{10... | collective-permute-start | bytes 1277960 | tf_op jit(solution)/shard_map/ppermute | solution.py:47
  6.8 2.1 %collective-permute-start.4 = (f32[26,1,8,512]{3,2,1,0:T(8,128)}, f32[26,1,8,512]{3,2,1,0:T(8,128)}, u32[]{:S(2)}, u32[]{:S(2)}) collective-permute-start(f32[26,1,8,512]{3,2,1,0:T(8,128)} %get-tuple-element.113), channel_id=1, source_target_pairs={{8,0},{16,8},{24,16},{0,24},{9,1},{17,9},{25,17},{1,25},{10,2},{18... | collective-permute-start | bytes 1277960 | tf_op jit(solution)/shard_map/ppermute | solution.py:50
  9.7 1.6 %fusion.4 = f32[1,8,8,512]{3,0,2,1:T(1,128)S(1)} fusion(pred[32,8,8,512]{3,2,1,0:T(8,128)(4,1)S(1)} %iota_compare_fusion.4, f32[32]{0:T(128)S(1)} %copy-done), kind=kOutput, calls=%fused_computation.22 | convolution fusion | flops 12582912 | bytes 1179776 | tf_op jit(solution)/shard_map/dot_general | solution.py:141
  11.4 1.0 multiply_reduce_fusion.7
  12.6 1.3 fusion.16
  14.3 1.8 %multiply_subtract_fusion = f32[19,8,8,512]{3,2,1,0:T(8,128)S(1)} fusion(f32[19,8,8,512]{3,2,1,0:T(8,128)S(1)} %constant_dynamic-update-slice_fusion, f32[19,8,8,512]{3,2,1,0:T(8,128)S(1)} %copy-done.7, f32[8,8,512]{2,1,0:T(8,128)S(1)} %get-tuple-element.77, f32[8,8,512]{2,1,0:T(8,128)S(1)} %get-tuple-element.81, f32[19]{0:T(128)S(1)} %copy-done.44, ...), kind=kLoop, calls=%fused_computation.48 | loop fusion | flops 12451840 | bytes 8126768 | tf_op jit(solution)/shard_map/sub | solution.py:86
  17.3 1.0 pad_maximum_fusion.10
  18.3 3.8 %collective-permute-start.1 = (f32[27,1,8,512]{3,2,1,0:T(8,128)}, f32[27,1,8,512]{3,2,1,0:T(8,128)}, u32[]{:S(2)}, u32[]{:S(2)}) collective-permute-start(f32[27,1,8,512]{3,2,1,0:T(8,128)} %get-tuple-element.111), channel_id=1, source_target_pairs={{8,0},{16,8},{24,16},{0,24},{9,1},{17,9},{25,17},{1,25},{10,2},{18... | collective-permute-start | bytes 1327112 | tf_op jit(solution)/shard_map/ppermute | solution.py:50
  22.1 7.0 %collective-permute-done.4 = f32[26,1,8,512]{3,2,1,0:T(8,128)} collective-permute-done((f32[26,1,8,512]{3,2,1,0:T(8,128)}, f32[26,1,8,512]{3,2,1,0:T(8,128)}, u32[]{:S(2)}, u32[]{:S(2)}) %collective-permute-start.4) | collective-permute-done | bytes 426016 | tf_op jit(solution)/shard_map/ppermute | solution.py:50
  29.1 4.5 %pad_maximum_fusion.5 = (f32[26,10,1,512]{3,2,1,0:T(1,128)S(1)}, f32[26,10,1,512]{3,2,1,0:T(1,128)S(1)}) fusion(f32[26,1,8,512]{3,2,1,0:T(8,128)} %collective-permute-done.4, f32[26,8,8,512]{3,2,1,0:T(8,128)} %copy-done.2, f32[26,1,8,512]{3,2,1,0:T(8,128)} %collective-permute-done.5), kind=kLoop, calls=%fused_computation.72 | loop fusion | flops 532480 | bytes 5324800 | tf_op jit(solution)/shard_map/concatenate | solution.py:51
  33.7 2.6 %collective-permute-start.6 = (f32[26,10,1,512]{3,2,1,0:T(1,128)S(1)}, f32[26,10,1,512]{3,2,1,0:T(1,128)S(1)}, u32[]{:S(2)}, u32[]{:S(2)}) collective-permute-start(f32[26,10,1,512]{3,2,1,0:T(1,128)S(1)} %get-tuple-element.109), channel_id=1, source_target_pairs={{1,0},{2,1},{3,2},{4,3},{5,4},{6,5},{7,6},{0,7},{9,8},{10,9},{11,1... | collective-permute-start | bytes 1597448 | tf_op jit(solution)/shard_map/ppermute | solution.py:50
  36.3 2.2 %collective-permute-done = f32[27,1,8,512]{3,2,1,0:T(8,128)} collective-permute-done((f32[27,1,8,512]{3,2,1,0:T(8,128)}, f32[27,1,8,512]{3,2,1,0:T(8,128)}, u32[]{:S(2)}, u32[]{:S(2)}) %collective-permute-start) | collective-permute-done | bytes 442400 | tf_op jit(solution)/shard_map/ppermute | solution.py:47
  38.5 8.1 %collective-permute-done.1 = f32[27,1,8,512]{3,2,1,0:T(8,128)} collective-permute-done((f32[27,1,8,512]{3,2,1,0:T(8,128)}, f32[27,1,8,512]{3,2,1,0:T(8,128)}, u32[]{:S(2)}, u32[]{:S(2)}) %collective-permute-start.1) | collective-permute-done | bytes 442400 | tf_op jit(solution)/shard_map/ppermute | solution.py:50
  46.6 2.2 %pad_maximum_fusion.4 = (f32[27,10,1,512]{3,2,1,0:T(1,128)S(1)}, f32[27,10,1,512]{3,2,1,0:T(1,128)S(1)}) fusion(f32[27,1,8,512]{3,2,1,0:T(8,128)} %collective-permute-done.1, f32[27,1,8,512]{3,2,1,0:T(8,128)} %collective-permute-done, f32[1,8,8,512]{3,2,1,0:T(8,128)S(1)} %copy-done.9, f32[7,8,8,512]{3,2,1,0:T(8,128)S(1)} %fusion.21, ...), kind=kLoop, calls=%fused_computation.71 | loop fusion | flops 1105920 | bytes 5529600 | tf_op jit(solution)/shard_map/slice | solution.py:48
  48.8 2.6 %collective-permute-start.3 = (f32[27,10,1,512]{3,2,1,0:T(1,128)S(1)}, f32[27,10,1,512]{3,2,1,0:T(1,128)S(1)}, u32[]{:S(2)}, u32[]{:S(2)}) collective-permute-start(f32[27,10,1,512]{3,2,1,0:T(1,128)S(1)} %get-tuple-element.103), channel_id=1, source_target_pairs={{1,0},{2,1},{3,2},{4,3},{5,4},{6,5},{7,6},{0,7},{9,8},{10,9},{11,1... | collective-permute-start | bytes 1658888 | tf_op jit(solution)/shard_map/ppermute | solution.py:50
  51.5 13.1 %select_maximum_fusion.6 = f32[26,10,10,514]{3,2,1,0:T(8,128)S(1)} fusion(f32[26,10,1,512]{3,2,1,0:T(1,128)S(1)} %collective-permute-done.6, f32[26,10,1,512]{3,2,1,0:T(1,128)S(1)} %collective-permute-done.7, f32[26,1,8,512]{3,2,1,0:T(8,128)} %collective-permute-done.4, f32[26,8,8,512]{3,2,1,0:T(8,128)S(1)} %copy-done.3, ...), kind=kLoop, calls=%fused_computation.11 | loop fusion | flops 16036800 | bytes 10670400 | tf_op jit(solution)/shard_map/concatenate | solution.py:51
  64.6 21.7 %select_maximum_fusion = f32[27,10,10,514]{3,2,1,0:T(8,128)S(1)} fusion(f32[27,10,1,512]{3,2,1,0:T(1,128)S(1)} %collective-permute-done.3, f32[27,10,1,512]{3,2,1,0:T(1,128)S(1)} %collective-permute-done.2, f32[27,1,8,512]{3,2,1,0:T(8,128)} %collective-permute-done.1, f32[27,1,8,512]{3,2,1,0:T(8,128)} %collective-permute-done, ...), kind=kLoop, calls=%fused_computation.4 | loop fusion | flops 22204800 | bytes 11080800 | tf_op jit(solution)/shard_map/concatenate | solution.py:51
  91.0 0.9 constant_dynamic-update-slice_fusion.68
  95.2 1.0 constant_dynamic-update-slice_fusion.43
  104.3 2.6 %fusion.7 = (f32[19,8,8,512]{3,2,1,0:T(8,128)S(1)}, f32[19,8,8,512]{3,2,1,0:T(8,128)S(1)}) fusion(f32[8,8,512]{2,1,0:T(8,128)S(1)} %get-tuple-element.47, f32[8,8,512]{2,1,0:T(8,128)S(1)} %get-tuple-element.40, f32[8,8,512]{2,1,0:T(8,128)S(1)} %get-tuple-element.43, f32[8,8,512]{2,1,0:T(8,128)S(1)} %get-tuple-element.41, f32[19]{0:T(128)S(1)} %copy-done.44, ...), kind=kLoop, calls=%fused_computation.25 | loop fusion | flops 25526272 | bytes 10355011 | tf_op jit(solution)/shard_map/transpose(jvp())/add_any | solution.py:82
  107.1 3.0 %multiply_reduce_fusion.3 = (f32[8,8,512]{2,1,0:T(8,128)}, f32[8,8,512]{2,1,0:T(8,128)S(1)}, f32[8,8,512]{2,1,0:T(8,128)}, f32[8,8,512]{2,1,0:T(8,128)S(1)}, f32[8,8,512]{2,1,0:T(8,128)}) fusion(f32[19,8,8,512]{3,2,1,0:T(8,128)S(1)} %get-tuple-element.48, f32[19]{0:T(128)S(1)} %copy-done.44, f32[19]{0:T(128)S(1)} %copy-done.46, f32[19]{0:T(128)S(1)} %copy-done.45, ...), kind=kLoop, calls=%fused_computation.39 | loop fusion | flops 14778368 | bytes 6291760 | tf_op jit(solution)/shard_map/transpose(jvp())/reduce_sum | solution.py:80
  110.2 1.6 %multiply_reduce_fusion.11 = (f32[8,8,512]{2,1,0:T(8,128)S(1)}, f32[8,8,512]{2,1,0:T(8,128)S(1)}, f32[8,8,512]{2,1,0:T(8,128)}, f32[8,8,512]{2,1,0:T(8,128)}, f32[8,8,512]{2,1,0:T(8,128)}, /*index=5*/f32[8,8,512]{2,1,0:T(8,128)}) fusion(f32[7,8,8,512]{3,2,1,0:T(8,128)S(1)} %get-tuple-element.86, f32[8,8,512]{2,1,0:T(8,128)S(1)} %get-tuple-element.39, ...), kind=kLoop, calls=%fused_computation.58 | loop fusion | flops 5308416 | bytes 2490592 | tf_op jit(solution)/shard_map/transpose(jvp())/reduce_sum | solution.py:89
  112.6 5.1 %fusion.18 = f32[32]{0:T(128)} fusion(pred[32,8,8,512]{3,2,1,0:T(8,128)(4,1)S(1)} %copy-done.35, f32[8,8,512,1]{2,1,0,3:T(8,128)S(1)} %get-tuple-element.33), kind=kOutput, calls=%fused_computation.55 | convolution fusion | flops 12582912 | bytes 1179776 | tf_op jit(solution)/shard_map/dot_general | solution.py:159
  117.7 13.4 %psum.14 = f32[32]{0:T(128)} all-reduce(f32[32]{0:T(128)} %fusion.18), channel_id=1, replica_groups=mesh['gx'=4,'gy'=8] {'gy'}, use_global_device_ids=true, to_apply=%region_23.24 | all-reduce | flops 32 | bytes 256 | tf_op jit(solution)/shard_map/psum | solution.py:160
  131.1 11.2 %psum.15 = f32[32]{0:T(128)} all-reduce(f32[32]{0:T(128)} %psum.14), channel_id=1, replica_groups=mesh['gx'=4,'gy'=8] {'gx'}, use_global_device_ids=true, to_apply=%region_24.25 | all-reduce | flops 32 | bytes 256 | tf_op jit(solution)/shard_map/psum | solution.py:160
  142.3 1.2 broadcast_multiply_fusion
  143.6 1.0 multiply_add_fusion.3
  144.7 1.1 multiply_add_fusion.1
  145.8 1.2 fusion.239
  147.3 2.5 %add_add_fusion = f32[19,8,8,512]{3,2,1,0:T(8,128)} fusion(f32[19,8,8,512]{3,2,1,0:T(8,128)S(1)} %copy-done.6, f32[19,8,8,512]{3,2,1,0:T(8,128)S(1)} %get-tuple-element.49, f32[8,8,512]{2,1,0:T(8,128)S(1)} %get-tuple-element.133, f32[8,8,512]{2,1,0:T(8,128)S(1)} %get-tuple-element.138, f32[8,8,512]{2,1,0:T(8,128)S(1)} %get-tuple-element.37, ...), kind=kLoop, calls=%fused_computation.36 | loop fusion | flops 6225920 | bytes 8126768 | tf_op jit(solution)/shard_map/transpose(jvp())/add_any | solution.py:68
  (211 shorter events, 19.4 us)
Async XLA Ops:
  0.6 9.1 %copy-start = (f32[32]{0:T(128)S(1)}, f32[32]{0:T(128)}, u32[]{:S(2)}) copy-start(f32[32]{0:T(128)} %param.23) | copy-start | bytes 388
  2.7 6.2 %copy-start.43 = (s32[8,8,512]{2,1,0:T(8,128)S(1)}, s32[8,8,512]{2,1,0:T(8,128)}, u32[]{:S(2)}) copy-start(s32[8,8,512]{2,1,0:T(8,128)} %param.25) | copy-start | bytes 393220
  2.7 6.8 %copy-start.36 = (f32[7,8,8,512]{3,2,1,0:T(8,128)S(1)}, f32[7,8,8,512]{3,2,1,0:T(8,128)}, u32[]{:S(2)}) copy-start(f32[7,8,8,512]{3,2,1,0:T(8,128)} %param.19) | copy-start | bytes 2752516
  2.7 6.8 %copy-start.47 = (f32[7]{0:T(128)S(1)}, f32[7]{0:T(128)}, u32[]{:S(2)}) copy-start(f32[7]{0:T(128)} %constant.97) | copy-start | bytes 88
  2.8 8.5 %copy-start.2 = (f32[26,8,8,512]{3,2,1,0:T(8,128)}, f32[26,8,8,512]{3,2,1,0:T(8,128)S(1)}, u32[]{:S(2)}) copy-start(f32[26,8,8,512]{3,2,1,0:T(8,128)S(1)} %constant_dynamic-update-slice_fusion.45) | copy-start | bytes 10223620
  3.8 18.4 %collective-permute-start.5 = (f32[26,1,8,512]{3,2,1,0:T(8,128)}, f32[26,1,8,512]{3,2,1,0:T(8,128)}, u32[]{:S(2)}, u32[]{:S(2)}) collective-permute-start(f32[26,1,8,512]{3,2,1,0:T(8,128)} %get-tuple-element.112), channel_id=1, source_target_pairs={{0,8},{8,16},{16,24},{24,0},{1,9},{9,17},{17,25},{25,1},{2,10},{10... | collective-permute-start | bytes 1277960 | tf_op jit(solution)/shard_map/ppermute | solution.py:47
  6.8 22.3 %collective-permute-start.4 = (f32[26,1,8,512]{3,2,1,0:T(8,128)}, f32[26,1,8,512]{3,2,1,0:T(8,128)}, u32[]{:S(2)}, u32[]{:S(2)}) collective-permute-start(f32[26,1,8,512]{3,2,1,0:T(8,128)} %get-tuple-element.113), channel_id=1, source_target_pairs={{8,0},{16,8},{24,16},{0,24},{9,1},{17,9},{25,17},{1,25},{10,2},{18... | collective-permute-start | bytes 1277960 | tf_op jit(solution)/shard_map/ppermute | solution.py:50
  18.3 20.2 %collective-permute-start = (f32[27,1,8,512]{3,2,1,0:T(8,128)}, f32[27,1,8,512]{3,2,1,0:T(8,128)}, u32[]{:S(2)}, u32[]{:S(2)}) collective-permute-start(f32[27,1,8,512]{3,2,1,0:T(8,128)} %get-tuple-element.110), channel_id=1, source_target_pairs={{0,8},{8,16},{16,24},{24,0},{1,9},{9,17},{17,25},{25,1},{2,10},{10... | collective-permute-start | bytes 1327112 | tf_op jit(solution)/shard_map/ppermute | solution.py:47
  18.3 28.2 %collective-permute-start.1 = (f32[27,1,8,512]{3,2,1,0:T(8,128)}, f32[27,1,8,512]{3,2,1,0:T(8,128)}, u32[]{:S(2)}, u32[]{:S(2)}) collective-permute-start(f32[27,1,8,512]{3,2,1,0:T(8,128)} %get-tuple-element.111), channel_id=1, source_target_pairs={{8,0},{16,8},{24,16},{0,24},{9,1},{17,9},{25,17},{1,25},{10,2},{18... | collective-permute-start | bytes 1327112 | tf_op jit(solution)/shard_map/ppermute | solution.py:50
  22.1 24.4 %copy-start.9 = (f32[1,8,8,512]{3,2,1,0:T(8,128)S(1)}, f32[1,8,8,512]{3,2,1,0:T(8,128)}, u32[]{:S(2)}) copy-start(f32[1,8,8,512]{3,2,1,0:T(8,128)} %copy-done.8) | copy-start | bytes 393220
  33.6 17.8 %collective-permute-start.7 = (f32[26,10,1,512]{3,2,1,0:T(1,128)S(1)}, f32[26,10,1,512]{3,2,1,0:T(1,128)S(1)}, u32[]{:S(2)}, u32[]{:S(2)}) collective-permute-start(f32[26,10,1,512]{3,2,1,0:T(1,128)S(1)} %get-tuple-element.108), channel_id=1, source_target_pairs={{0,1},{1,2},{2,3},{3,4},{4,5},{5,6},{6,7},{7,0},{8,9},{9,10},{10,1... | collective-permute-start | bytes 1597448 | tf_op jit(solution)/shard_map/ppermute | solution.py:47
  33.7 17.8 %collective-permute-start.6 = (f32[26,10,1,512]{3,2,1,0:T(1,128)S(1)}, f32[26,10,1,512]{3,2,1,0:T(1,128)S(1)}, u32[]{:S(2)}, u32[]{:S(2)}) collective-permute-start(f32[26,10,1,512]{3,2,1,0:T(1,128)S(1)} %get-tuple-element.109), channel_id=1, source_target_pairs={{1,0},{2,1},{3,2},{4,3},{5,4},{6,5},{7,6},{0,7},{9,8},{10,9},{11,1... | collective-permute-start | bytes 1597448 | tf_op jit(solution)/shard_map/ppermute | solution.py:50
  36.3 15.1 %copy-start.3 = (f32[26,8,8,512]{3,2,1,0:T(8,128)S(1)}, f32[26,8,8,512]{3,2,1,0:T(8,128)}, u32[]{:S(2)}) copy-start(f32[26,8,8,512]{3,2,1,0:T(8,128)} %copy-done.2) | copy-start | bytes 10223620
  48.8 15.8 %collective-permute-start.2 = (f32[27,10,1,512]{3,2,1,0:T(1,128)S(1)}, f32[27,10,1,512]{3,2,1,0:T(1,128)S(1)}, u32[]{:S(2)}, u32[]{:S(2)}) collective-permute-start(f32[27,10,1,512]{3,2,1,0:T(1,128)S(1)} %get-tuple-element.102), channel_id=1, source_target_pairs={{0,1},{1,2},{2,3},{3,4},{4,5},{5,6},{6,7},{7,0},{8,9},{9,10},{10,1... | collective-permute-start | bytes 1658888 | tf_op jit(solution)/shard_map/ppermute | solution.py:47
  48.8 15.7 %collective-permute-start.3 = (f32[27,10,1,512]{3,2,1,0:T(1,128)S(1)}, f32[27,10,1,512]{3,2,1,0:T(1,128)S(1)}, u32[]{:S(2)}, u32[]{:S(2)}) collective-permute-start(f32[27,10,1,512]{3,2,1,0:T(1,128)S(1)} %get-tuple-element.103), channel_id=1, source_target_pairs={{1,0},{2,1},{3,2},{4,3},{5,4},{6,5},{7,6},{0,7},{9,8},{10,9},{11,1... | collective-permute-start | bytes 1658888 | tf_op jit(solution)/shard_map/ppermute | solution.py:50
  64.5 21.9 %copy-start.10 = (f32[19,8,8,512]{3,2,1,0:T(8,128)S(1)}, f32[19,8,8,512]{3,2,1,0:T(8,128)}, u32[]{:S(2)}) copy-start(f32[19,8,8,512]{3,2,1,0:T(8,128)} %param.20) | copy-start | bytes 7471108
  64.5 21.9 %copy-start.19 = (f32[7,8,8,512]{3,2,1,0:T(8,128)S(1)}, f32[7,8,8,512]{3,2,1,0:T(8,128)}, u32[]{:S(2)}) copy-start(f32[7,8,8,512]{3,2,1,0:T(8,128)} %param.21) | copy-start | bytes 2752516
  94.5 9.7 %copy-start.5 = (f32[19,8,8,512]{3,2,1,0:T(8,128)}, f32[19,8,8,512]{3,2,1,0:T(8,128)S(1)}, u32[]{:S(2)}) copy-start(f32[19,8,8,512]{3,2,1,0:T(8,128)S(1)} %get-tuple-element.87) | copy-start | bytes 7471108
  103.6 6.5 %copy-start.11 = (f32[8,8,512]{2,1,0:T(8,128)}, f32[8,8,512]{2,1,0:T(8,128)S(1)}, u32[]{:S(2)}) copy-start(f32[8,8,512]{2,1,0:T(8,128)S(1)} %get-tuple-element.40) | copy-start | bytes 393220
  103.6 8.3 %copy-start.13 = (f32[8,8,512]{2,1,0:T(8,128)}, f32[8,8,512]{2,1,0:T(8,128)S(1)}, u32[]{:S(2)}) copy-start(f32[8,8,512]{2,1,0:T(8,128)S(1)} %get-tuple-element.41) | copy-start | bytes 393220
  104.2 5.9 %copy-start.20 = (f32[8,8,512]{2,1,0:T(8,128)}, f32[8,8,512]{2,1,0:T(8,128)S(1)}, u32[]{:S(2)}) copy-start(f32[8,8,512]{2,1,0:T(8,128)S(1)} %get-tuple-element.47) | copy-start | bytes 393220
  104.2 5.9 %copy-start.33 = (f32[8,8,512]{2,1,0:T(8,128)}, f32[8,8,512]{2,1,0:T(8,128)S(1)}, u32[]{:S(2)}) copy-start(f32[8,8,512]{2,1,0:T(8,128)S(1)} %get-tuple-element.45) | copy-start | bytes 393220
  104.3 7.6 %copy-start.30 = (f32[8,8,512]{2,1,0:T(8,128)}, f32[8,8,512]{2,1,0:T(8,128)S(1)}, u32[]{:S(2)}) copy-start(f32[8,8,512]{2,1,0:T(8,128)S(1)} %get-tuple-element.44) | copy-start | bytes 393220
  111.9 31.7 %copy-start.12 = (f32[8,8,512]{2,1,0:T(8,128)S(1)}, f32[8,8,512]{2,1,0:T(8,128)}, u32[]{:S(2)}) copy-start(f32[8,8,512]{2,1,0:T(8,128)} %copy-done.11) | copy-start | bytes 393220
  111.9 31.7 %copy-start.17 = (f32[8,8,512]{2,1,0:T(8,128)S(1)}, f32[8,8,512]{2,1,0:T(8,128)}, u32[]{:S(2)}) copy-start(f32[8,8,512]{2,1,0:T(8,128)} %copy-done.15) | copy-start | bytes 393220
  112.6 31.0 %copy-start.14 = (f32[8,8,512]{2,1,0:T(8,128)S(1)}, f32[8,8,512]{2,1,0:T(8,128)}, u32[]{:S(2)}) copy-start(f32[8,8,512]{2,1,0:T(8,128)} %copy-done.13) | copy-start | bytes 393220
  112.6 33.2 %copy-start.23 = (f32[8,8,512]{2,1,0:T(8,128)S(1)}, f32[8,8,512]{2,1,0:T(8,128)}, u32[]{:S(2)}) copy-start(f32[8,8,512]{2,1,0:T(8,128)} %copy-done.22) | copy-start | bytes 393220
  117.7 29.2 %copy-start.21 = (f32[8,8,512]{2,1,0:T(8,128)S(1)}, f32[8,8,512]{2,1,0:T(8,128)}, u32[]{:S(2)}) copy-start(f32[8,8,512]{2,1,0:T(8,128)} %copy-done.20) | copy-start | bytes 393220
  117.7 29.2 %copy-start.27 = (f32[8,8,512]{2,1,0:T(8,128)S(1)}, f32[8,8,512]{2,1,0:T(8,128)}, u32[]{:S(2)}) copy-start(f32[8,8,512]{2,1,0:T(8,128)} %copy-done.26) | copy-start | bytes 393220
  142.3 4.7 %copy-start.38 = (f32[8,8,512]{2,1,0:T(8,128)S(1)}, f32[8,8,512]{2,1,0:T(8,128)}, u32[]{:S(2)}) copy-start(f32[8,8,512]{2,1,0:T(8,128)} %get-tuple-element.32) | copy-start | bytes 393220
  142.3 4.7 %copy-start.39 = (f32[8,8,512]{2,1,0:T(8,128)S(1)}, f32[8,8,512]{2,1,0:T(8,128)}, u32[]{:S(2)}) copy-start(f32[8,8,512]{2,1,0:T(8,128)} %get-tuple-element.26) | copy-start | bytes 393220
  142.3 4.7 %copy-start.40 = (f32[8,8,512]{2,1,0:T(8,128)S(1)}, f32[8,8,512]{2,1,0:T(8,128)}, u32[]{:S(2)}) copy-start(f32[8,8,512]{2,1,0:T(8,128)} %get-tuple-element.28) | copy-start | bytes 393220
  (42 other events, 106.8 us)
